TPU v7x, 32 devices: a whole 2x2x4 slice. The times are simulated.
32 devices in a mesh: ep: 16 (over z, x, core), etp: 2 (over y).
Axes of the slice: x: 2, y: 2, z: 4, core: 2. Of those that a mesh axis runs over, the one named last changes fastest.
Arguments:
- tokens: bfloat16 [2048, 4096], P('ep', 'etp'), may hold values from -6 to 6
- grad_out: bfloat16 [2048, 4096], P('ep', 'etp'), may hold values from -1.5 to 1.5
- gates: float32 [2048, 8], P('ep'), may hold values from 0.05 to 0.5
- expert_ids: int32 [2048, 8], P('ep'), may hold values from 0 to 15, all different within a row; in each aligned block of 128 rows (0 to 127, 128 to 255, ...) at most 72 rows name the same one
- gate_proj: bfloat16 [16, 4096, 1536], P('ep', None, 'etp'), may hold values from -0.09375 to 0.09375
- up_proj: bfloat16 [16, 4096, 1536], P('ep', None, 'etp'), may hold values from -0.09375 to 0.09375
- down_proj: bfloat16 [16, 1536, 4096], P('ep', 'etp'), may hold values from -0.15625 to 0.15625
Outputs:
- layer_out: bfloat16 [2048, 4096], P('ep', 'etp')
- token_grad: bfloat16 [2048, 4096], P('ep', 'etp')
- slot_gate_grad: float32 [2048, 8], P('ep')
Inputs may be any that keep to these rules, and one draw needn't show every extreme that they name: `expert_ids`: each row names 8 different experts. Within the rows of one index of ep (aligned blocks of 128 rows) no expert is named by more than 72 rows, and in every draw some expert is named by exactly 72 rows of some block.
All inputs are finite; a program needn't handle non-finite values.
Results may differ from a plain program's by a relative error of at most 0.015.
Values may be sent and summed in bfloat16 or wider, within the bound.
A program may use at most 128 MiB of HBM per device.

v0:
```python
import jax
import jax.numpy as jnp
from jax import lax
from jax.sharding import PartitionSpec as P


def expert_rows(token_rows, signal_rows, gate_mat, up_mat, down_mat):
    gate_pre = jnp.dot(token_rows, gate_mat, preferred_element_type=jnp.float32)
    up_pre = jnp.dot(token_rows, up_mat, preferred_element_type=jnp.float32)
    sigmoid_gate = jax.nn.sigmoid(gate_pre)
    hidden = (gate_pre * sigmoid_gate * up_pre).astype(jnp.bfloat16)
    part_out = jnp.dot(hidden, down_mat, preferred_element_type=jnp.float32).astype(jnp.bfloat16)
    contract = (((1,), (1,)), ((), ()))
    hidden_grad = lax.dot_general(
        signal_rows, down_mat, contract, preferred_element_type=jnp.float32
    )
    gate_grad = (
        hidden_grad * up_pre * sigmoid_gate * (1.0 + gate_pre * (1.0 - sigmoid_gate))
    ).astype(jnp.bfloat16)
    up_grad = (hidden_grad * gate_pre * sigmoid_gate).astype(jnp.bfloat16)
    part_in = lax.dot_general(gate_grad, gate_mat, contract, preferred_element_type=jnp.float32)
    part_in = part_in + lax.dot_general(
        up_grad, up_mat, contract, preferred_element_type=jnp.float32
    )
    return (part_out, part_in.astype(jnp.bfloat16))


def local(tokens, grad_out, gates, expert_ids, gate_proj, up_proj, down_proj):
    tok_rows, quarter = tokens.shape
    fanout = expert_ids.shape[1]
    groups = lax.axis_size("etp")
    sources = lax.axis_size("ep")
    capacity = min(
        tok_rows, tok_rows * fanout // sources + max(1, tok_rows * fanout // (8 * sources))
    )
    copies = tok_rows * fanout
    full_width = quarter * groups
    flat_ids = expert_ids.reshape(copies)
    onehot = (flat_ids[:, None] == jnp.arange(sources, dtype=jnp.int32)[None, :]).astype(jnp.int32)
    before = jnp.cumsum(onehot, axis=0) - onehot
    slot_pos = jnp.sum(before * onehot, axis=1)
    target = flat_ids * capacity + slot_pos
    owner_row = jnp.arange(copies, dtype=jnp.int32) // fanout
    gate_flat = gates.reshape(copies)

    def place(values, columns):
        empty = jnp.zeros((sources * capacity, columns), jnp.bfloat16)
        return empty.at[target].set(values).reshape(sources, capacity, columns)

    full_tok, full_grad = (
        lax.all_gather(tokens, "etp", axis=1, tiled=True),
        lax.all_gather(grad_out, "etp", axis=1, tiled=True),
    )
    token_buf = place(full_tok[owner_row], full_width)
    signal_buf = place(
        (gate_flat[:, None] * full_grad[owner_row].astype(jnp.float32)).astype(jnp.bfloat16),
        full_width,
    )
    token_in, signal_in = (
        lax.all_to_all(token_buf, "ep", split_axis=0, concat_axis=0, tiled=True),
        lax.all_to_all(signal_buf, "ep", split_axis=0, concat_axis=0, tiled=True),
    )
    recv_rows = sources * capacity
    token_in = token_in.reshape(recv_rows, full_width)
    signal_in = signal_in.reshape(recv_rows, full_width)
    gate_mat = gate_proj[0]
    up_mat = up_proj[0]
    down_mat = down_proj[0]
    part_out, part_in = expert_rows(token_in, signal_in, gate_mat, up_mat, down_mat)
    out_sum, in_sum = (
        lax.psum_scatter(part_out, "etp", scatter_dimension=1, tiled=True).astype(jnp.float32),
        lax.psum_scatter(part_in, "etp", scatter_dimension=1, tiled=True).astype(jnp.float32),
    )
    out_copy = out_sum.astype(jnp.bfloat16).reshape(sources, capacity, quarter)
    in_copy = in_sum.astype(jnp.bfloat16).reshape(sources, capacity, quarter)
    out_back, in_back = (
        lax.all_to_all(out_copy, "ep", split_axis=0, concat_axis=0, tiled=True),
        lax.all_to_all(in_copy, "ep", split_axis=0, concat_axis=0, tiled=True),
    )
    out_tok = out_back.reshape(sources * capacity, quarter)[target].reshape(
        tok_rows, fanout, quarter
    )
    in_tok = in_back.reshape(sources * capacity, quarter)[target].reshape(tok_rows, fanout, quarter)
    layer_out = jnp.sum(gates[:, :, None] * out_tok.astype(jnp.float32), axis=1).astype(
        jnp.bfloat16
    )
    token_grad = jnp.sum(in_tok.astype(jnp.float32), axis=1).astype(jnp.bfloat16)
    partial_scores = jnp.einsum("tkd,td->tk", out_tok, grad_out, preferred_element_type=jnp.float32)
    slot_gate_grad = lax.psum(partial_scores, "etp")
    return (layer_out, token_grad, slot_gate_grad)


def solution(mesh):
    in_specs = (
        P("ep", "etp"),
        P("ep", "etp"),
        P("ep", None),
        P("ep", None),
        P("ep", None, "etp"),
        P("ep", None, "etp"),
        P("ep", "etp", None),
    )
    out_specs = (P("ep", "etp"), P("ep", "etp"), P("ep", None))
    return jax.shard_map(local, mesh=mesh, in_specs=in_specs, out_specs=out_specs, check_vma=False)
```

profile of v0, /device:TPU:11, one launch (start us, length us, event | category | flops | bytes accessed | tf_op | source)
XLA Modules:
  0.0 779.0 jit_solution(3242398556894386793)
XLA Ops:
  7.2 0.7 all-gather.3.cloned.1.call-update
  7.9 0.7 broadcast_multiply_fusion
  8.6 0.8 copy.15
  9.8 4.5 reduce-window.6
  14.8 17.2 %all-gather.3.cloned.1.call-done = bf16[128,4096]{1,0:T(8,128)(2,1)} async-done(((bf16[128,2048]{1,0:T(8,128)(2,1)}), bf16[128,4096]{1,0:T(8,128)(2,1)}) %all-gather.3.cloned.1.call-update) | async-done | bytes 1048592 | tf_op jit(solution)/shard_map/all_gather | solution.py:51
  32.0 16.4 %gather_fusion = bf16[1024,4096]{1,0:T(8,128)(2,1)} fusion(bf16[128,4096]{1,0:T(8,128)(2,1)} %all-gather.3.cloned.1.call-done, s32[1024]{0:T(1024)S(1)} %broadcast_clamp_fusion.1), kind=kCustom, calls=%fused_computation | custom fusion | bytes 16781312 | tf_op jit(solution)/shard_map/gather | solution.py:54
  48.5 18.8 %scatter_custom_fusion = bf16[1152,4096]{1,0:T(8,128)(2,1)} fusion(s32[1024]{0:T(1024)S(1)} %bitcast.65, bf16[1024,4096]{1,0:T(8,128)(2,1)} %gather_fusion, bf16[]{:T(256)} %constant.26.clone.1), kind=kCustom, calls=%fused_computation.23 | custom fusion | bytes 9437696 | tf_op jit(solution)/shard_map/scatter | solution.py:48
  67.3 6.4 all-to-all-start
  73.7 0.7 all-gather.5.cloned.1.call-update
  74.6 22.4 %all-gather.5.cloned.1.call-done = bf16[128,4096]{1,0:T(8,128)(2,1)} async-done(((bf16[128,2048]{1,0:T(8,128)(2,1)}), bf16[128,4096]{1,0:T(8,128)(2,1)}) %all-gather.5.cloned.1.call-update) | async-done | bytes 1048592 | tf_op jit(solution)/shard_map/all_gather | solution.py:52
  97.0 16.4 %gather_fusion.2 = bf16[1024,4096]{1,0:T(8,128)(2,1)} fusion(bf16[128,4096]{1,0:T(8,128)(2,1)} %all-gather.5.cloned.1.call-done, s32[1024]{0:T(1024)S(1)} %broadcast_clamp_fusion.1), kind=kCustom, calls=%fused_computation.2 | custom fusion | bytes 16781312 | tf_op jit(solution)/shard_map/gather | solution.py:56
  113.4 18.7 %scatter_custom_fusion.1 = bf16[1152,4096]{1,0:T(8,128)(2,1)} fusion(s32[1024]{0:T(1024)S(1)} %bitcast.66, bf16[1024,4096]{1,0:T(8,128)(2,1)} %gather_fusion.2, f32[1024]{0:T(1024)S(1)} %mul.69, bf16[]{:T(256)} %constant.26.clone.1), kind=kCustom, calls=%fused_computation.9 | custom fusion | flops 12582912 | bytes 17829890 | tf_op jit(solution)/shard_map/scatter | solution.py:48
  132.1 146.3 %all-to-all-done = bf16[16,72,4096]{2,1,0:T(8,128)(2,1)} async-done(((bf16[16,72,4096]{2,1,0:T(8,128)(2,1)}), bf16[16,72,4096]{2,1,0:T(8,128)(2,1)}, u32[]{:S(2)}, u32[]{:S(2)}) %all-to-all-start) | async-done | bytes 9437216 | tf_op jit(solution)/shard_map/all_to_all | solution.py:60
  278.5 4.9 all-to-all-start.2
  283.4 12.0 %fusion.10 = f32[1152,768]{1,0:T(8,128)S(1)} fusion(bf16[1152,4096]{1,0:T(8,128)(2,1)} %bitcast.6, bf16[1,4096,768]{2,1,0:T(8,128)(2,1)} %param.11), kind=kOutput, calls=%fused_computation.20 | convolution fusion | flops 7247757312 | bytes 19267584 | tf_op jit(solution)/shard_map/dot_general | solution.py:8
  295.5 13.2 %fusion.6 = f32[1152,768]{1,0:T(8,128)S(1)} fusion(bf16[1152,4096]{1,0:T(8,128)(2,1)} %bitcast.6, bf16[1,4096,768]{2,1,0:T(8,128)(2,1)} %param.12), kind=kOutput, calls=%fused_computation.16 | convolution fusion | flops 7247757312 | bytes 19267584 | tf_op jit(solution)/shard_map/dot_general | solution.py:9
  308.7 1.7 copy-done.4
  310.4 9.8 %convolution_convert_fusion = bf16[1152,4096]{1,0:T(8,128)(2,1)} fusion(bf16[1,768,4096]{2,1,0:T(8,128)(2,1)S(1)} %bitcast.71, f32[1152,768]{1,0:T(8,128)S(1)} %fusion.6, f32[1152,768]{1,0:T(8,128)S(1)} %fusion.10), kind=kOutput, calls=%fused_computation.8 | convolution fusion | flops 7257784320 | bytes 22806528 | tf_op jit(solution)/shard_map/dot_general | solution.py:12
  320.5 167.7 %all-to-all-done.2 = bf16[16,72,4096]{2,1,0:T(8,128)(2,1)} async-done(((bf16[16,72,4096]{2,1,0:T(8,128)(2,1)}), bf16[16,72,4096]{2,1,0:T(8,128)(2,1)}, u32[]{:S(2)}, u32[]{:S(2)}) %all-to-all-start.2) | async-done | bytes 9437216 | tf_op jit(solution)/shard_map/all_to_all | solution.py:61
  488.2 13.3 %fusion.2 = f32[1152,768]{1,0:T(8,128)} fusion(bf16[1152,4096]{1,0:T(8,128)(2,1)} %bitcast.14, bf16[1,768,4096]{2,1,0:T(8,128)(2,1)} %param.13), kind=kOutput, calls=%fused_computation.12 | convolution fusion | flops 7247757312 | bytes 19267584 | tf_op jit(solution)/shard_map/dot_general | solution.py:14
  501.5 16.3 %fusion.8 = f32[1152,4096]{1,0:T(8,128)} fusion(bf16[1,4096,768]{2,1,0:T(8,128)(2,1)} %param.11, f32[1152,768]{1,0:T(8,128)S(1)} %copy-done.3, f32[1152,768]{1,0:T(8,128)} %fusion.2, f32[1152,768]{1,0:T(8,128)S(1)} %copy-done.5), kind=kOutput, calls=%fused_computation.18 | convolution fusion | flops 7256604672 | bytes 35782656 | tf_op jit(solution)/shard_map/dot_general | solution.py:21
  517.8 17.0 %add_convert_fusion = bf16[1152,4096]{1,0:T(8,128)(2,1)} fusion(f32[1152,4096]{1,0:T(8,128)} %fusion.8, bf16[1,4096,768]{2,1,0:T(8,128)(2,1)} %param.12, f32[1152,768]{1,0:T(8,128)} %fusion.2, f32[1152,768]{1,0:T(8,128)} %copy-done.2), kind=kOutput, calls=%fused_computation.6 | convolution fusion | flops 7262502912 | bytes 41680896 | tf_op jit(solution)/shard_map/dot_general | solution.py:22
  534.8 4.9 all-to-all-start.1
  539.7 104.3 %reduce-scatter.5.cloned.1.call-done = bf16[1152,2048]{1,0:T(8,128)(2,1)} async-done(((bf16[1152,4096]{1,0:T(8,128)(2,1)}), bf16[1152,2048]{1,0:T(8,128)(2,1)}) %reduce-scatter.5.cloned.1.call-update) | async-done | bytes 4718608 | tf_op jit(solution)/shard_map/reduce_scatter | solution.py:72
  644.0 6.8 all-to-all-start.3
  650.8 11.8 %gather_fusion.1 = bf16[1024,2048]{1,0:T(8,128)(2,1)} fusion(bf16[1152,2048]{1,0:T(8,128)(2,1)} %bitcast.11, s32[1024]{0:T(1024)S(1)} %broadcast_clamp_fusion), kind=kCustom, calls=%fused_computation.1 | custom fusion | bytes 8392704 | tf_op jit(solution)/shard_map/gather | solution.py:80
  662.6 4.9 fusion.15
  667.6 4.8 psum.7
  672.3 7.3 multiply_reduce_fusion
  679.7 74.7 %all-to-all-done.3 = bf16[16,72,2048]{2,1,0:T(8,128)(2,1)} async-done(((bf16[16,72,2048]{2,1,0:T(8,128)(2,1)}), bf16[16,72,2048]{2,1,0:T(8,128)(2,1)}, u32[]{:S(2)}, u32[]{:S(2)}) %all-to-all-start.3) | async-done | bytes 4718624 | tf_op jit(solution)/shard_map/all_to_all | solution.py:78
  754.3 11.8 %gather_fusion.3 = bf16[1024,2048]{1,0:T(8,128)(2,1)} fusion(bf16[1152,2048]{1,0:T(8,128)(2,1)} %bitcast.16, s32[1024]{0:T(1024)S(1)} %broadcast_clamp_fusion), kind=kCustom, calls=%fused_computation.3 | custom fusion | bytes 8392704 | tf_op jit(solution)/shard_map/gather | solution.py:83
  766.1 5.9 bitcast_reduce_fusion
  (43 shorter events, 1.6 us)
Async XLA Ops:
  7.2 24.9 %all-gather.3.cloned.1.call-start = ((), (), s32[]{:S(2)}) async-start(), calls=%async_computation.6 | async-start | bytes 1572864 | tf_op jit(solution)/shard_map/all_gather | solution.py:51
  67.2 7.1 copy-start.1
  67.3 211.2 %all-to-all-start = ((bf16[16,72,4096]{2,1,0:T(8,128)(2,1)}), bf16[16,72,4096]{2,1,0:T(8,128)(2,1)}, u32[]{:S(2)}, u32[]{:S(2)}) async-start(bf16[16,72,4096]{2,1,0:T(8,128)(2,1)} %bitcast.58), calls=%async_computation | async-start | bytes 18874368 | tf_op jit(solution)/shard_map/all_to_all | solution.py:60
  73.6 23.4 %all-gather.5.cloned.1.call-start = ((), (), s32[]{:S(2)}) async-start(), calls=%async_computation.8 | async-start | bytes 1572864 | tf_op jit(solution)/shard_map/all_gather | solution.py:52
  278.5 209.7 %all-to-all-start.2 = ((bf16[16,72,4096]{2,1,0:T(8,128)(2,1)}), bf16[16,72,4096]{2,1,0:T(8,128)(2,1)}, u32[]{:S(2)}, u32[]{:S(2)}) async-start(bf16[16,72,4096]{2,1,0:T(8,128)(2,1)} %bitcast.57), calls=%async_computation.3 | async-start | bytes 18874368 | tf_op jit(solution)/shard_map/all_to_all | solution.py:61
  283.4 251.4 %reduce-scatter.3.cloned.1.call-start = ((), (), s32[]{:S(2)}) async-start(), calls=%async_computation.7 | async-start | bytes 14155776 | tf_op jit(solution)/shard_map/reduce_scatter | solution.py:71
  283.4 27.0 %slice-start = ((s8[6291456]{0:T(1024)(128)(4,1)}), s8[4194304]{0:T(1024)(128)(4,1)S(1)}, s32[]{:S(2)}) async-start(s8[6291456]{0:T(1024)(128)(4,1)} %bitcast.70), calls=%async_computation.10 | async-start | bytes 8388608
  295.4 13.2 %copy-start.2 = (f32[1152,768]{1,0:T(8,128)}, f32[1152,768]{1,0:T(8,128)S(1)}, u32[]{:S(2)}) copy-start(f32[1152,768]{1,0:T(8,128)S(1)} %fusion.10) | copy-start | bytes 10616836
  295.5 15.0 %slice-start.1 = ((s8[6291456]{0:T(1024)(128)(4,1)}), s8[2097152]{0:T(1024)(128)(4,1)S(1)}, s32[]{:S(2)}) async-start(s8[6291456]{0:T(1024)(128)(4,1)} %bitcast.70), calls=%async_computation.11 | async-start | bytes 4194304
  308.7 1.7 copy-start.4
  320.3 323.7 %reduce-scatter.5.cloned.1.call-start = ((), (), s32[]{:S(2)}) async-start(), calls=%async_computation.9 | async-start | bytes 14155776 | tf_op jit(solution)/shard_map/reduce_scatter | solution.py:72
  488.2 13.3 %copy-start.3 = (f32[1152,768]{1,0:T(8,128)S(1)}, f32[1152,768]{1,0:T(8,128)}, u32[]{:S(2)}) copy-start(f32[1152,768]{1,0:T(8,128)} %copy-done.2) | copy-start | bytes 10616836
  488.2 13.3 %copy-start.5 = (f32[1152,768]{1,0:T(8,128)S(1)}, f32[1152,768]{1,0:T(8,128)}, u32[]{:S(2)}) copy-start(f32[1152,768]{1,0:T(8,128)} %copy-done.4) | copy-start | bytes 10616836
  534.8 109.2 %all-to-all-start.1 = ((bf16[16,72,2048]{2,1,0:T(8,128)(2,1)}), bf16[16,72,2048]{2,1,0:T(8,128)(2,1)}, u32[]{:S(2)}, u32[]{:S(2)}) async-start(bf16[16,72,2048]{2,1,0:T(8,128)(2,1)} %bitcast.59), calls=%async_computation.2 | async-start | bytes 9437184 | tf_op jit(solution)/shard_map/all_to_all | solution.py:77
  644.0 110.3 %all-to-all-start.3 = ((bf16[16,72,2048]{2,1,0:T(8,128)(2,1)}), bf16[16,72,2048]{2,1,0:T(8,128)(2,1)}, u32[]{:S(2)}, u32[]{:S(2)}) async-start(bf16[16,72,2048]{2,1,0:T(8,128)(2,1)} %bitcast.60), calls=%async_computation.5 | async-start | bytes 9437184 | tf_op jit(solution)/shard_map/all_to_all | solution.py:78
  650.8 11.8 %copy-start = (bf16[128,2048]{1,0:T(8,128)(2,1)S(1)}, bf16[128,2048]{1,0:T(8,128)(2,1)}, u32[]{:S(2)}) copy-start(bf16[128,2048]{1,0:T(8,128)(2,1)} %param.8) | copy-start | bytes 1572868
Sparse Core Ops, SparseCore 0:
  9.5 22.4 all-gather.2
  76.0 20.9 all-gather.4
  320.4 110.1 reduce-scatter.2
  534.9 109.0 reduce-scatter.4
where the time goes:
time: 787 us; the launch traced here: 779 us
  waiting for transfers between devices  534 us (68%)
  matrix products  86.4 us (11%)
  local copies, waits for them, and re-layouts  78.7 us (10%)
  other arithmetic  37.2 us (5%)
  starting transfers between devices  23.3 us (3%)
  between operations  14.4 us (2%)
    all_to_all x1, waiting for transfers between devices, local(): lax.all_to_all(signal_buf, 'ep', split_axis=0, concat_axis=0, tiled=True)  168 us
    all_to_all x1, waiting for transfers between devices, local(): lax.all_to_all(token_buf, 'ep', split_axis=0, concat_axis=0, tiled=True)  146 us
    reduce_scatter x1, waiting for transfers between devices, local(): lax.psum_scatter(part_in, 'etp', scatter_dimension=1, tiled=True)  104 us
    all_to_all x1, waiting for transfers between devices, local(): lax.all_to_all(in_copy, 'ep', split_axis=0, concat_axis=0, tiled=True)  74.7 us
    all_gather x1, waiting for transfers between devices, local(): lax.all_gather(grad_out, 'etp', axis=1, tiled=True)  22.4 us
    scatter x1, local copies, waits for them, and re-layouts, place(): return empty.at[target].set(values).reshape(sources, capacity, columns)  18.8 us
    scatter x1, other arithmetic, place(): return empty.at[target].set(values).reshape(sources, capacity, columns)  18.7 us
    all_gather x1, waiting for transfers between devices, local(): lax.all_gather(tokens, 'etp', axis=1, tiled=True)  17.2 us
  transfers between devices with their start and end apart: 8, of which 6 were waited for; matrix products, arithmetic and copies ran while one was open for 19% of the time, Pallas kernels for 0%

commit v1 on v0

v1 whole, which is shorter than its diff:
```python
import functools
import math

import jax
import jax.numpy as jnp
import numpy as np
from jax import lax
from jax.experimental import pallas as pl
from jax.experimental.pallas import tpu as pltpu
from jax.sharding import PartitionSpec as P

BF = jnp.bfloat16
F32 = jnp.float32
MESH = pl.DeviceIdType.MESH


class Place:
    def __init__(self, ring, groups):
        self.ring, self.groups = ring, groups
        self.depth = math.gcd(ring, 4)
        self.cols = ring // self.depth
        me = lax.axis_index("ep")
        self.g = lax.axis_index("etp")
        self.core = lax.rem(me, 2)
        chip = me // 2
        x, z = lax.rem(chip, self.cols), chip // self.cols
        self.p = x * self.depth + z + lax.rem(x, 2) * (self.depth - 1 - 2 * z)

    def at(self, offset):
        return lax.rem(self.p + offset + self.ring, self.ring)

    def chip(self, offset):
        pos = self.at(offset)
        x, t = pos // self.depth, lax.rem(pos, self.depth)
        z = t + lax.rem(x, 2) * (self.depth - 1 - 2 * t)
        return ((z * self.cols + x) * 2 + self.core, self.g)

    def sibling(self):
        return (lax.axis_index("ep") + 1 - 2 * self.core, self.g)

    def group(self, j):
        return lax.rem(self.g + j, self.groups)

    def partner(self, j):
        return (lax.axis_index("ep"), self.group(j))

    def greet(self, with_sibling):
        barrier = pltpu.get_barrier_semaphore()
        others = [self.chip(1), self.chip(-1)] + [self.partner(j) for j in range(1, self.groups)]
        if with_sibling:
            others.append(self.sibling())
        for other in others:
            pl.semaphore_signal(barrier, inc=1, device_id=other, device_id_type=MESH)
        pl.semaphore_wait(barrier, len(others))


def remote(src, dst, send, recv, where):
    return pltpu.make_async_remote_copy(
        src_ref=src, dst_ref=dst, send_sem=send, recv_sem=recv, device_id=where, device_id_type=MESH
    )


def gather_kernel(
    ring, groups, tok_ref, grad_ref, tok, tok_sib, grad, grad_sib, local_sem, first, rings, fans, late
):
    at = Place(ring, groups)
    at.greet(True)
    g = at.g
    sib = at.sibling()
    own_tok = pltpu.make_async_copy(tok_ref, tok.at[g, at.p], local_sem.at[0])
    own_grad = pltpu.make_async_copy(grad_ref, grad.at[g, at.p], local_sem.at[1])
    own_tok.start()
    own_grad.start()
    heads = []
    for j in range(1, groups):
        head = remote(
            grad_ref, grad.at[g, at.p], first.at[0, j - 1], first.at[1, j - 1], at.partner(j)
        )
        head.start()
        heads.append(head)
    own_tok.wait()

    def back(d, s):
        return at.at(-s if d == 0 else s)

    fan_y, fan_s, fan_t = {}, {}, {}

    def fan_tok(s):
        for d in range(2):
            b = back(d, s)
            fan_y[s, d] = []
            for j in range(1, groups):
                c = remote(
                    tok.at[g, b, d],
                    tok.at[g, b, d],
                    fans.at[0, j, d, s],
                    fans.at[1, j, d, s],
                    at.partner(j),
                )
                c.start()
                fan_y[s, d].append(c)

    def fan_grad(s):
        for d in range(2):
            b = back(d, s)
            c = remote(
                grad.at[:, b, d], grad_sib.at[:, b, d], fans.at[0, 0, d, s], fans.at[1, 0, d, s], sib
            )
            c.start()
            fan_s[s, d] = c

    def fan_late(s):
        for d in range(2):
            b = back(d, s)
            for c in fan_y[s, d]:
                c.wait_recv()
            c = remote(tok.at[:, b, d], tok_sib.at[:, b, d], late.at[0, d, s], late.at[1, d, s], sib)
            c.start()
            fan_t[s, d] = c

    hops = {}

    def hop(kind, d, s):
        b = back(d, s - 1)
        block = tok.at[g, b, d] if kind == 0 else grad.at[:, b, d]
        if s > 1:
            hops[kind, d, s - 1].wait_recv()
        if s < ring:
            c = remote(
                block,
                block,
                rings.at[0, kind, d, s - 1],
                rings.at[1, kind, d, s - 1],
                at.chip(1 if d == 0 else -1),
            )
            c.start()
            hops[kind, d, s] = c

    for s in range(1, ring + 1):
        hop(0, 0, s)
        hop(0, 1, s)
        if s == 1:
            own_grad.wait()
            for head in heads:
                head.wait_recv()
        if s < ring:
            fan_tok(s - 1)
        hop(1, 0, s)
        hop(1, 1, s)
        if s < ring:
            fan_grad(s - 1)
        if s >= 2:
            fan_late(s - 2)
    fan_tok(ring - 1)
    fan_grad(ring - 1)
    fan_late(ring - 1)
    for c in list(fan_s.values()) + list(fan_t.values()):
        c.wait()
    for group in fan_y.values():
        for c in group:
            c.wait_send()
    for c in list(hops.values()) + heads:
        c.wait_send()


def gather(tokens, grad_out, ring, groups):
    rows, width = tokens.shape
    half = rows // 2
    full = jax.ShapeDtypeStruct((groups, ring, 2, half, width), BF)
    dma = pltpu.SemaphoreType.DMA
    hbm = pl.BlockSpec(memory_space=pltpu.HBM)
    return pl.pallas_call(
        functools.partial(gather_kernel, ring, groups),
        out_shape=(full,) * 4,
        in_specs=[hbm, hbm],
        out_specs=(hbm,) * 4,
        scratch_shapes=[
            dma((2,)),
            dma((2, groups - 1)),
            dma((2, 2, 2, ring - 1)),
            dma((2, groups, 2, ring)),
            dma((2, 2, ring)),
        ],
        compiler_params=pltpu.CompilerParams(collective_id=0, has_side_effects=True),
    )(tokens.reshape(2, half, width), grad_out.reshape(2, half, width))


def scatter_kernel(
    ring, groups, s_out, s_in, res_out, res_in, v_out, v_in, r_out, r_in, y_in, y_out, loads, rings, ys, tail
):
    at = Place(ring, groups)
    g = at.g
    half = v_in.shape[2]

    def dest(d, s):
        return at.at(-s if d == 0 else s)

    load_out, load_in, swap = {}, {}, {}
    for s in range(1, ring + 1):
        for d in range(2):
            b = dest(d, s)
            load_out[s, d] = pltpu.make_async_copy(
                s_out.at[:, b, d], v_out.at[:, b, d], loads.at[0, d, s - 1]
            )
            load_in[s, d] = pltpu.make_async_copy(s_in.at[g, b, d], v_in.at[b, d], loads.at[1, d, s - 1])
            load_out[s, d].start()
            load_in[s, d].start()
    at.greet(False)
    for s in range(1, ring + 1):
        for d in range(2):
            b = dest(d, s)
            swap[s, d] = []
            for j in range(1, groups):
                c = remote(
                    s_in.at[at.group(j), b, d],
                    y_in.at[j - 1, b, d],
                    ys.at[0, j - 1, d, s - 1],
                    ys.at[1, j - 1, d, s - 1],
                    at.partner(j),
                )
                c.start()
                swap[s, d].append(c)

    def total(target, others):
        @pl.loop(0, half // 16)
        def _(i):
            rows = pl.ds(pl.multiple_of(i * 16, 16), 16)
            acc = target[rows, :].astype(F32)
            for other in others:
                acc = acc + other[rows, :].astype(F32)
            target[rows, :] = acc.astype(BF)

    hop_out, hop_in = {}, {}
    for s in range(1, ring + 1):
        for d in range(2):
            b = dest(d, s)
            load_out[s, d].wait()
            if s > 1:
                hop_out[s - 1, d].wait_recv()
                for q in range(groups):
                    total(v_out.at[q, b, d], [r_out.at[d, s - 2, q]])
            if s < ring:
                c = remote(
                    v_out.at[:, b, d],
                    r_out.at[d, s - 1],
                    rings.at[0, 0, d, s - 1],
                    rings.at[1, 0, d, s - 1],
                    at.chip(1 if d == 0 else -1),
                )
                c.start()
                hop_out[s, d] = c
        if s == ring:
            ends = []
            for d in range(2):
                for j in range(1, groups):
                    c = remote(
                        v_out.at[at.group(j), at.p, d],
                        y_out.at[j - 1, d],
                        tail.at[0, j - 1, d],
                        tail.at[1, j - 1, d],
                        at.partner(j),
                    )
                    c.start()
                    ends.append(c)
        for d in range(2):
            b = dest(d, s)
            load_in[s, d].wait()
            others = []
            for c in swap[s, d]:
                c.wait_recv()
            others = [y_in.at[j - 1, b, d] for j in range(1, groups)]
            if s > 1:
                hop_in[s - 1, d].wait_recv()
                others.append(r_in.at[d, s - 2])
            total(v_in.at[b, d], others)
            if s < ring:
                c = remote(
                    v_in.at[b, d],
                    r_in.at[d, s - 1],
                    rings.at[0, 1, d, s - 1],
                    rings.at[1, 1, d, s - 1],
                    at.chip(1 if d == 0 else -1),
                )
                c.start()
                hop_in[s, d] = c
    for d in range(2):
        res_in[d] = v_in[at.p, d]
    for c in ends:
        c.wait_recv()
    for d in range(2):
        total(v_out.at[g, at.p, d], [y_out.at[j - 1, d] for j in range(1, groups)])
        res_out[d] = v_out[g, at.p, d]
    for c in list(hop_out.values()) + list(hop_in.values()) + ends:
        c.wait_send()
    for group in swap.values():
        for c in group:
            c.wait_send()


def scatter(s_out, s_in):
    groups, ring, _, half, width = s_out.shape
    res = jax.ShapeDtypeStruct((2, half, width), BF)
    dma = pltpu.SemaphoreType.DMA
    hbm = pl.BlockSpec(memory_space=pltpu.HBM)
    vmem = pl.BlockSpec(memory_space=pltpu.VMEM)
    out, inn = pl.pallas_call(
        functools.partial(scatter_kernel, ring, groups),
        out_shape=(res, res),
        in_specs=[hbm, hbm],
        out_specs=(vmem, vmem),
        scratch_shapes=[
            pltpu.VMEM((groups, ring, 2, half, width), BF),
            pltpu.VMEM((ring, 2, half, width), BF),
            pltpu.VMEM((2, ring - 1, groups, half, width), BF),
            pltpu.VMEM((2, ring - 1, half, width), BF),
            pltpu.VMEM((groups - 1, ring, 2, half, width), BF),
            pltpu.VMEM((groups - 1, 2, half, width), BF),
            dma((2, 2, ring)),
            dma((2, 2, 2, ring - 1)),
            dma((2, groups - 1, 2, ring)),
            dma((2, groups - 1, 2)),
        ],
        compiler_params=pltpu.CompilerParams(
            collective_id=1, has_side_effects=True, vmem_limit_bytes=60 << 20
        ),
    )(s_out, s_in)
    return out.reshape(2 * half, width), inn.reshape(2 * half, width)


def dot(a, b):
    return lax.dot_general(a, b, (((1,), (0,)), ((), ())), preferred_element_type=F32)


def dot_t(a, b):
    return lax.dot_general(a, b, (((1,), (1,)), ((), ())), preferred_element_type=F32)


def expert_kernel(groups, adding, gate_ref, tok, grad, gate_w, up_w, down_w, *rest):
    if adding:
        add_out, add_in, out, inn, score = rest
    else:
        out, inn, score = rest
    width = tok.shape[2]
    cuts = [slice(g * width, (g + 1) * width) for g in range(groups)]
    gate_pre = sum(dot(tok[g], gate_w[cuts[g], :]) for g in range(groups))
    up_pre = sum(dot(tok[g], up_w[cuts[g], :]) for g in range(groups))
    raw = sum(dot_t(grad[g], down_w[:, cuts[g]]) for g in range(groups))
    gate = gate_ref[...]
    sig = jax.nn.sigmoid(gate_pre)
    act = gate_pre * sig
    hidden = act * up_pre
    score[...] = jnp.sum(hidden * raw, axis=1, keepdims=True)
    hidden = (hidden * gate).astype(BF)
    back = raw * gate
    gate_grad = (back * up_pre * sig * (1.0 + gate_pre * (1.0 - sig))).astype(BF)
    up_grad = (back * act).astype(BF)
    for g in range(groups):
        res = dot(hidden, down_w[:, cuts[g]])
        if adding:
            res = res + add_out[g].astype(F32)
        out[g] = res.astype(BF)
        res = dot_t(gate_grad, gate_w[cuts[g], :]) + dot_t(up_grad, up_w[cuts[g], :])
        if adding:
            res = res + add_in[g].astype(F32)
        inn[g] = res.astype(BF)


def expert(gate, tok, grad, gate_proj, up_proj, down_proj, added=()):
    groups, count, width = tok.shape
    tile = 256
    slab = pl.BlockSpec((groups, tile, width), lambda i: (0, i, 0))
    column = pl.BlockSpec((tile, 1), lambda i: (i, 0))

    def fixed(w):
        return pl.BlockSpec((None,) + w.shape[1:], lambda i: (0, 0, 0), pipeline_mode=pl.Buffered(1))

    full = jax.ShapeDtypeStruct(tok.shape, BF)
    hid = gate_proj.shape[2]
    return pl.pallas_call(
        functools.partial(expert_kernel, groups, bool(added)),
        grid=(count // tile,),
        out_shape=(full, full, jax.ShapeDtypeStruct((count, 1), F32)),
        in_specs=[column, slab, slab, fixed(gate_proj), fixed(up_proj), fixed(down_proj)]
        + [slab] * len(added),
        out_specs=(slab, slab, column),
        input_output_aliases={6: 0, 7: 1} if added else {},
        cost_estimate=pl.CostEstimate(
            flops=12 * count * groups * width * hid, bytes_accessed=8 * count * groups * width, transcendentals=count * hid
        ),
        compiler_params=pltpu.CompilerParams(vmem_limit_bytes=60 << 20),
    )(gate, tok, grad, gate_proj, up_proj, down_proj, *added)


def local(tokens, grad_out, gates, expert_ids, gate_proj, up_proj, down_proj):
    rows, width = tokens.shape
    groups = lax.axis_size("etp")
    experts = lax.axis_size("ep")
    ring = experts // 2
    core = lax.rem(lax.axis_index("ep"), 2)
    depth = math.gcd(ring, 4)
    cols = ring // depth
    order = np.zeros(ring, np.int32)
    for pos in range(ring):
        x, t = pos // depth, pos % depth
        order[pos] = (t if x % 2 == 0 else depth - 1 - t) * cols + x
    inverse = np.argsort(order)
    count = ring * rows

    onehot = expert_ids[:, :, None] == jnp.arange(experts, dtype=jnp.int32)[None, None, :]
    table = jnp.sum(jnp.where(onehot, gates[:, :, None], 0.0), axis=1)
    mine = lax.all_to_all(table.T, "ep", split_axis=0, concat_axis=0, tiled=True)
    mine = mine.reshape(ring, 2, rows)
    mine = jnp.stack([mine[int(c)] for c in order]).transpose(1, 0, 2)
    mine = jnp.where(core == 0, mine, mine[::-1])

    tok_own, tok_sib, grad_own, grad_sib = gather(tokens, grad_out, ring, groups)
    flat = (groups, count, width)
    swap = [(i, i ^ 1) for i in range(experts)]
    weights = (gate_proj, up_proj, down_proj)
    out, inn, score_sib = expert(
        mine[1].reshape(count, 1), tok_sib.reshape(flat), grad_sib.reshape(flat), *weights
    )
    got = (lax.ppermute(out, "ep", swap), lax.ppermute(inn, "ep", swap))
    out, inn, score_own = expert(
        mine[0].reshape(count, 1), tok_own.reshape(flat), grad_own.reshape(flat), *weights, added=got
    )
    scores = [score_own.reshape(ring, rows), score_sib.reshape(ring, rows)]
    shape = (groups, ring, 2, rows // 2, width)
    layer_out, token_grad = scatter(out.reshape(shape), inn.reshape(shape))

    score = jnp.stack(scores)
    score = jnp.where(core == 0, score, score[::-1]).transpose(1, 0, 2)
    score = jnp.stack([score[int(c)] for c in inverse]).reshape(experts, rows)
    score = lax.all_to_all(score, "ep", split_axis=0, concat_axis=0, tiled=True)
    score = lax.psum(score, "etp")
    picked = jnp.sum(jnp.where(onehot, score.T[:, None, :], 0.0), axis=2)
    return layer_out, token_grad, picked


def solution(mesh):
    in_specs = (
        P("ep", "etp"),
        P("ep", "etp"),
        P("ep", None),
        P("ep", None),
        P("ep", None, "etp"),
        P("ep", None, "etp"),
        P("ep", "etp", None),
    )
    out_specs = (P("ep", "etp"), P("ep", "etp"), P("ep", None))
    return jax.shard_map(local, mesh=mesh, in_specs=in_specs, out_specs=out_specs, check_vma=False)
```

time: 787 us -> 452 us (0.57)
  waiting for transfers between devices: 534 us -> 22.7 us
  Pallas kernels: 0 us -> 394 us
  matrix products: 86.4 us -> 0 us
  local copies, waits for them, and re-layouts: 78.7 us -> 6.5 us
  other arithmetic: 37.2 us -> 4.43 us
  between operations: 14.4 us -> 0.74 us
  starting transfers between devices: 23.3 us -> 12 us
    pallas_call x0 -> x4, Pallas kernels: none -> 394 us  [the longest x1 166 us: gather(): pl.pallas_call(functools.partial(gather_kernel, ring, groups), out_shape=...]
    all_to_all x4 -> x2, waiting for transfers between devices: 389 us -> 0.01 us  [the longest x1 0.01 us: local(): lax.all_to_all(table.T, 'ep', split_axis=0, concat_axis=0, tiled=True)]
    reduce_scatter x2 -> x0, waiting for transfers between devices: 104 us -> none  [the longest x1 104 us: local(): lax.psum_scatter(part_in, 'etp', scatter_dimension=1, tiled=True)]
    dot_general x7 -> x0, matrix products: 86.4 us -> none  [the longest x1 17 us: expert_rows(): lax.dot_general(up_grad, up_mat, contract, preferred_element_type=jnp.flo...]
    gather x4 -> x0, local copies, waits for them, and re-layouts: 56.4 us -> none  [the longest x1 16.4 us: local(): token_buf = place(full_tok[owner_row], full_width)]
    all_gather x2 -> x0, waiting for transfers between devices: 39.7 us -> none  [the longest x1 22.4 us: local(): lax.all_gather(grad_out, 'etp', axis=1, tiled=True)]
    ppermute x0 -> x2, waiting for transfers between devices: none -> 22.7 us  [local(): got = (lax.ppermute(out, 'ep', swap), lax.ppermute(inn, 'ep', swap))]
    scatter x1 -> x0, local copies, waits for them, and re-layouts: 18.8 us -> none  [place(): return empty.at[target].set(values).reshape(sources, capacity, columns)]
  transfers between devices with their start and end apart: 8 -> 4, of which waited for: 6 -> 2; matrix products, arithmetic and copies ran while one was open for 19% -> 1% of each run, Pallas kernels for 0% -> 66%
where the time goes in v1:
time: 452 us; the launch traced here: 445 us
  Pallas kernels  394 us (87%)
  waiting for transfers between devices  22.7 us (5%)
  starting transfers between devices  12 us (3%)
  local copies, waits for them, and re-layouts  6.5 us (1%)
    pallas_call x1, Pallas kernels, gather(): pl.pallas_call(functools.partial(gather_kernel, ring, groups), out_shape=...  166 us
    pallas_call x1, Pallas kernels, scatter(): pl.pallas_call(functools.partial(scatter_kernel, ring, groups), out_shape...  127 us
    pallas_call x2, Pallas kernels, expert(): pl.pallas_call(functools.partial(expert_kernel, groups, bool(added)), gri...  102 us
    ppermute x2, waiting for transfers between devices, local(): got = (lax.ppermute(out, 'ep', swap), lax.ppermute(inn, 'ep', swap))  22.7 us
  transfers between devices with their start and end apart: 4, of which 2 were waited for; matrix products, arithmetic and copies ran while one was open for 1% of the time, Pallas kernels for 66%

profile of v1, /device:TPU:11, one launch (start us, length us, event | category | flops | bytes accessed | tf_op | source)
XLA Modules:
  0.0 445.0 jit_solution(10993504322086029968)
XLA Ops:
  0.6 1.3 select_reduce_fusion.1
  1.9 6.6 %all-to-all-start = ((f32[16,1,128]{2,1,0:T(1,128)}), f32[16,1,128]{2,1,0:T(1,128)S(1)}, u32[]{:S(2)}, u32[]{:S(2)}) async-start(f32[16,1,128]{2,1,0:T(1,128)} %bitcast.2), calls=%async_computation | async-start | bytes 16384 | tf_op jit(solution)/shard_map/all_to_all | solution.py:411
  8.5 166.0 %shard_map.94 = (bf16[2,8,2,64,2048]{4,3,2,1,0:T(8,128)(2,1)}, bf16[2,8,2,64,2048]{4,3,2,1,0:T(8,128)(2,1)}, bf16[2,8,2,64,2048]{4,3,2,1,0:T(8,128)(2,1)}, bf16[2,8,2,64,2048]{4,3,2,1,0:T(8,128)(2,1)}) custom-call(bf16[2,64,2048]{2,1,0:T(8,128)(2,1)} %bitcast.37, bf16[2,64,2048]{2,1,0:T(8,128)(2,1)} %bitcast.38), custom_call_target="tpu_custom_call" | custom-call | tf_op jit(solution)/shard_map/pallas_call | solution.py:172
  174.5 0.0 all-to-all-done
  174.6 1.0 copy.58.gate_ref
  175.6 50.3 %shard_map.95 = (bf16[2,1024,2048]{2,1,0:T(8,128)(2,1)}, bf16[2,1024,2048]{2,1,0:T(8,128)(2,1)}, f32[1024,1]{1,0:T(8,128)}) custom-call(f32[1024,1]{1,0:T(8,128)} %copy.58.gate_ref, bf16[2,1024,2048]{2,1,0:T(8,128)(2,1)} %bitcast.58, bf16[2,1024,2048]{2,1,0:T(8,128)(2,1)} %bitcast.59, bf16[1,4096,768]{2,1,0:T(8,128)(2,1)} %gate_w.3, ...), custom_call_target="tpu_custom_call" | custom-call | flops 38654705664 | bytes 33554432 | tf_op jit(solution)/shard_map/pallas_call | solution.py:379
  225.9 0.1 collective-permute-start
  226.0 0.4 collective-permute-start.1
  226.4 1.0 copy.59.gate_ref
  227.4 1.2 reduce.1
  228.6 10.7 %collective-permute-done.rest_0_ = bf16[2,1024,2048]{2,1,0:T(8,128)(2,1)} collective-permute-done((bf16[2,1024,2048]{2,1,0:T(8,128)(2,1)}, bf16[2,1024,2048]{2,1,0:T(8,128)(2,1)}, u32[]{:S(2)}, u32[]{:S(2)}) %collective-permute-start) | collective-permute-done | bytes 8388640 | tf_op jit(solution)/shard_map/ppermute | solution.py:423
  239.4 12.0 %collective-permute-done.1.rest_1_ = bf16[2,1024,2048]{2,1,0:T(8,128)(2,1)} collective-permute-done((bf16[2,1024,2048]{2,1,0:T(8,128)(2,1)}, bf16[2,1024,2048]{2,1,0:T(8,128)(2,1)}, u32[]{:S(2)}, u32[]{:S(2)}) %collective-permute-start.1) | collective-permute-done | bytes 8388640 | tf_op jit(solution)/shard_map/ppermute | solution.py:423
  251.4 51.5 %shard_map.96 = (bf16[2,1024,2048]{2,1,0:T(8,128)(2,1)}, bf16[2,1024,2048]{2,1,0:T(8,128)(2,1)}, f32[1024,1]{1,0:T(8,128)}) custom-call(f32[1024,1]{1,0:T(8,128)} %copy.59.gate_ref, bf16[2,1024,2048]{2,1,0:T(8,128)(2,1)} %bitcast.56, bf16[2,1024,2048]{2,1,0:T(8,128)(2,1)} %bitcast.57, ...), custom_call_target="tpu_custom_call", output_to_operand_aliasing={{0}: (6, {}), {1}: (7, {})} | custom-call | flops 38654705664 | bytes 33554432 | tf_op jit(solution)/shard_map/pallas_call | solution.py:379
  302.9 1.2 reduce
  304.2 0.6 copy.60
  304.8 4.9 %all-to-all-start.1 = ((f32[16,1,128]{2,1,0:T(1,128)}), f32[16,1,128]{2,1,0:T(1,128)S(1)}, u32[]{:S(2)}, u32[]{:S(2)}) async-start(f32[16,1,128]{2,1,0:T(1,128)} %bitcast.27), calls=%async_computation.1 | async-start | bytes 16384 | tf_op jit(solution)/shard_map/all_to_all | solution.py:434
  309.7 0.0 copy-start
  309.7 126.5 %shard_map.97 = (bf16[2,64,2048]{2,1,0:T(8,128)(2,1)}, bf16[2,64,2048]{2,1,0:T(8,128)(2,1)}) custom-call(bf16[2,8,2,64,2048]{4,3,2,1,0:T(8,128)(2,1)} %bitcast.21.s_out, bf16[2,8,2,64,2048]{4,3,2,1,0:T(8,128)(2,1)} %bitcast.22.s_in), custom_call_target="tpu_custom_call" | custom-call | tf_op jit(solution)/shard_map/pallas_call | solution.py:306
  436.2 0.0 all-to-all-done.1
  436.2 4.4 psum.7
  440.7 0.0 copy-done
  440.7 0.6 select_reduce_fusion
  441.3 1.9 copy.66
  443.2 1.9 copy.67
  (9 shorter events, 0.1 us)
Async XLA Ops:
  1.9 172.6 %all-to-all-start = ((f32[16,1,128]{2,1,0:T(1,128)}), f32[16,1,128]{2,1,0:T(1,128)S(1)}, u32[]{:S(2)}, u32[]{:S(2)}) async-start(f32[16,1,128]{2,1,0:T(1,128)} %bitcast.2), calls=%async_computation | async-start | bytes 16384 | tf_op jit(solution)/shard_map/all_to_all | solution.py:411
  225.9 13.5 %collective-permute-start = (bf16[2,1024,2048]{2,1,0:T(8,128)(2,1)}, bf16[2,1024,2048]{2,1,0:T(8,128)(2,1)}, u32[]{:S(2)}, u32[]{:S(2)}) collective-permute-start(bf16[2,1024,2048]{2,1,0:T(8,128)(2,1)} %get-tuple-element.19), channel_id=1, source_target_pairs={{0,2},{2,0},{4,6},{6,4},{8,10},{10,8},{12,14},{14,12},{16,18},{18,... | collective-permute-start | bytes 25165832 | tf_op jit(solution)/shard_map/ppermute | solution.py:423
  226.0 25.4 %collective-permute-start.1 = (bf16[2,1024,2048]{2,1,0:T(8,128)(2,1)}, bf16[2,1024,2048]{2,1,0:T(8,128)(2,1)}, u32[]{:S(2)}, u32[]{:S(2)}) collective-permute-start(bf16[2,1024,2048]{2,1,0:T(8,128)(2,1)} %get-tuple-element.20), channel_id=1, source_target_pairs={{0,2},{2,0},{4,6},{6,4},{8,10},{10,8},{12,14},{14,12},{16,18},{18,... | collective-permute-start | bytes 25165832 | tf_op jit(solution)/shard_map/ppermute | solution.py:423
  304.8 131.4 %all-to-all-start.1 = ((f32[16,1,128]{2,1,0:T(1,128)}), f32[16,1,128]{2,1,0:T(1,128)S(1)}, u32[]{:S(2)}, u32[]{:S(2)}) async-start(f32[16,1,128]{2,1,0:T(1,128)} %bitcast.27), calls=%async_computation.1 | async-start | bytes 16384 | tf_op jit(solution)/shard_map/all_to_all | solution.py:434
  309.7 131.0 %copy-start = (s32[128,8]{0,1:T(8,128)S(1)}, s32[128,8]{0,1:T(8,128)}, u32[]{:S(2)}) copy-start(s32[128,8]{0,1:T(8,128)} %param.10) | copy-start | bytes 12292
